TPU v7x, 32 devices: a whole 2x2x4 slice. The times are simulated.
32 devices in a mesh: row: 16 (over z, x, core), col: 2 (over y).
Axes of the slice: x: 2, y: 2, z: 4, core: 2. Of those that a mesh axis runs over, the one named last changes fastest.
Arguments:
- teacher_hidden: bfloat16 [512, 4608], P('row', 'col'), as said below
- student_hidden: bfloat16 [512, 3584], P('row', 'col'), as said below
- teacher_embed: bfloat16 [16384, 4608], P(('row', 'col')), may hold values from -0.4861359 to 0.4861359
- student_embed: bfloat16 [16384, 3584], P(('row', 'col')), may hold values from -0.5512263 to 0.5512263
Outputs:
- divergence: float32 [512], P(('row', 'col'))
- mean_divergence: float32 [], replicated
Inputs may be any that keep to these rules, and one draw needn't show every extreme that they name: `teacher_hidden`: entries of order one; a few rows may be far larger. `student_hidden`: entries of order one; a few rows may be far larger.
All inputs are finite; a program needn't handle non-finite values.
Results may differ from a plain program's by a relative error of at most 0.0003.
Values may be sent and summed in bfloat16 or wider, within the bound.
A program may use at most 64 MiB of HBM per device.

v0:
```python
import jax
import jax.numpy as jnp
from jax import lax
from jax.sharding import PartitionSpec as P


def block_stats(logit_teacher, logit_student):
    top_teacher = jnp.max(logit_teacher, 1)
    top_student = jnp.max(logit_student, 1)
    weights = jnp.exp(logit_teacher - top_teacher[:, None])
    sum_teacher = jnp.sum(weights, 1)
    cross_term = jnp.sum(weights * (logit_teacher - logit_student), 1)
    sum_student = jnp.sum(jnp.exp(logit_student - top_student[:, None]), 1)
    return (top_teacher, sum_teacher, cross_term, top_student, sum_student)


def per_device(teacher_hidden, student_hidden, teacher_embed, student_embed):
    tokens = teacher_hidden.shape[0] * lax.axis_size("row")
    full_teacher, full_student = (
        lax.all_gather(teacher_hidden, "col", axis=1, tiled=True),
        lax.all_gather(student_hidden, "col", axis=1, tiled=True),
    )
    logit_teacher = jnp.einsum(
        "td,vd->tv",
        lax.all_gather(full_teacher, "row", axis=0, tiled=True),
        teacher_embed,
        preferred_element_type=jnp.float32,
    )
    logit_student = jnp.einsum(
        "td,vd->tv",
        lax.all_gather(full_student, "row", axis=0, tiled=True),
        student_embed,
        preferred_element_type=jnp.float32,
    )
    current = block_stats(logit_teacher, logit_student)
    partial_stats = tuple((fresh_rows for fresh_rows in current))
    top_teacher, sum_teacher, cross_term, top_student, sum_student = partial_stats
    high_teacher, high_student = lax.pmax((top_teacher, top_student), ("row", "col"))
    teacher_scale = jnp.exp(top_teacher - high_teacher)
    student_scale = jnp.exp(top_student - high_student)
    sum_teacher, cross_term, sum_student = lax.psum(
        (sum_teacher * teacher_scale, cross_term * teacher_scale, sum_student * student_scale),
        ("row", "col"),
    )
    top_teacher, top_student = (high_teacher, high_student)
    divergence = (
        cross_term / sum_teacher
        - top_teacher
        - jnp.log(sum_teacher)
        + top_student
        + jnp.log(sum_student)
    )
    mean_divergence = jnp.mean(divergence)
    own_count = tokens // (lax.axis_size("row") * lax.axis_size("col"))
    own_block = lax.axis_index("row") * lax.axis_size("col") + lax.axis_index("col")
    return (lax.dynamic_slice_in_dim(divergence, own_block * own_count, own_count), mean_divergence)


def solution(mesh):
    return jax.shard_map(
        per_device,
        mesh=mesh,
        in_specs=(
            P("row", "col"),
            P("row", "col"),
            P(("row", "col"), None),
            P(("row", "col"), None),
        ),
        out_specs=(P(("row", "col")), P()),
        check_vma=False,
    )
```

profile of v0, /device:TPU:0, one launch (start us, length us, event | category | flops | bytes accessed | tf_op | source)
XLA Modules:
  0.0 213.5 jit_solution(12317152551401748478)
XLA Ops:
  7.2 0.0 all-gather.5.cloned.1.call-start
  7.2 8.6 %all_gather.14 = bf16[32,3584]{1,0:T(8,128)(2,1)} all-gather(bf16[32,1792]{1,0:T(8,128)(2,1)} %param.5), channel_id=1, replica_groups=mesh['row'=16,'col'=2] {'col'}, dimensions={1}, use_global_device_ids=true | all-gather | bytes 344064 | tf_op jit(solution)/shard_map/all_gather | solution.py:21
  15.9 0.0 all-gather.5.cloned.1.call-update
  15.9 0.0 all-gather.3.cloned.1.call-start
  15.9 6.1 %all_gather.12 = bf16[32,4608]{1,0:T(8,128)(2,1)} all-gather(bf16[32,2304]{1,0:T(8,128)(2,1)} %param.4), channel_id=1, replica_groups=mesh['row'=16,'col'=2] {'col'}, dimensions={1}, use_global_device_ids=true | all-gather | bytes 442368 | tf_op jit(solution)/shard_map/all_gather | solution.py:20
  22.1 0.0 all-gather.3.cloned.1.call-update
  22.1 41.9 %all-gather.5.cloned.1.call-done = bf16[512,3584]{1,0:T(8,128)(2,1)} async-done(((bf16[32,3584]{1,0:T(8,128)(2,1)}), bf16[512,3584]{1,0:T(8,128)(2,1)}) %all-gather.5.cloned.1.call-update) | async-done | bytes 3670032 | tf_op jit(solution)/shard_map/all_gather | solution.py:31
  64.0 5.3 %fusion.5 = (f32[512]{0:T(512)S(1)}, f32[512,512]{0,1:T(8,128)S(1)}) fusion(bf16[512,3584]{1,0:T(8,128)(2,1)} %all-gather.5.cloned.1.call-done, bf16[512,3584]{1,0:T(8,128)(2,1)} %param.7), kind=kOutput, calls=%fused_computation.11 | convolution fusion | flops 1879309824 | bytes 8390656 | tf_op jit(solution)/shard_map/td,vd->tv/dot_general | solution.py:29
  69.2 48.9 %all-gather.3.cloned.1.call-done = bf16[512,4608]{1,0:T(8,128)(2,1)} async-done(((bf16[32,4608]{1,0:T(8,128)(2,1)}), bf16[512,4608]{1,0:T(8,128)(2,1)}) %all-gather.3.cloned.1.call-update) | async-done | bytes 4718608 | tf_op jit(solution)/shard_map/all_gather | solution.py:25
  118.1 5.9 %fusion.4 = (f32[512]{0:T(512)S(1)}, f32[512,512]{0,1:T(8,128)S(1)}) fusion(bf16[512,4608]{1,0:T(8,128)(2,1)} %all-gather.3.cloned.1.call-done, bf16[512,4608]{1,0:T(8,128)(2,1)} %param.6), kind=kOutput, calls=%fused_computation.10 | convolution fusion | flops 2416180736 | bytes 10487808 | tf_op jit(solution)/shard_map/td,vd->tv/dot_general | solution.py:23
  124.0 39.2 %all-reduce.1 = (f32[512]{0:T(512)S(1)}, f32[512]{0:T(512)S(1)}) all-reduce(f32[512]{0:T(512)S(1)} %get-tuple-element.16, f32[512]{0:T(512)S(1)} %get-tuple-element.14), channel_id=1, replica_groups=mesh['row'=16,'col'=2] {'row','col'}, use_global_device_ids=true, to_apply=%region_7.0 | all-reduce | flops 1024 | bytes 8192 | tf_op jit(solution)/shard_map/pmax | solution.py:38
  163.3 0.4 multiply_reduce_fusion
  163.7 40.0 %all-reduce = (f32[512]{0:T(512)S(1)}, f32[512]{0:T(512)S(1)}, f32[512]{0:T(512)S(1)}) all-reduce(f32[512]{0:T(512)S(1)} %get-tuple-element.18, f32[512]{0:T(512)S(1)} %get-tuple-element.13, f32[512]{0:T(512)S(1)} %get-tuple-element.12), channel_id=1, replica_groups=mesh['row'=16,'col'=2] {'row','col'}, use_global_device_ids=true, to_apply=%region_9.0 | all-reduce | flops 1536 | bytes 12288 | tf_op jit(solution)/shard_map/psum | solution.py:41
  203.7 0.6 fusion.3
  204.3 0.6 dynamic_slice.3
  (1 shorter events, 0.0 us)
Async XLA Ops:
  7.2 56.8 %all-gather.5.cloned.1.call-start = ((), (), s32[]{:S(2)}) async-start(), calls=%async_computation.1 | async-start | bytes 3899392 | tf_op jit(solution)/shard_map/all_gather | solution.py:31
  15.9 102.2 %all-gather.3.cloned.1.call-start = ((), (), s32[]{:S(2)}) async-start(), calls=%async_computation | async-start | bytes 5013504 | tf_op jit(solution)/shard_map/all_gather | solution.py:25
Sparse Core Ops, SparseCore 0:
  16.0 47.9 all-gather.4
  66.3 51.8 all-gather.2
where the time goes:
time: 214 us
  blocking collectives  94 us (44%)
  waiting for transfers between devices  90.8 us (42%)
  between operations  15.8 us (7%)
  matrix products  11.2 us (5%)
    all_gather x1, waiting for transfers between devices, per_device(): lax.all_gather(full_teacher, 'row', axis=0, tiled=True)  48.9 us
    all_gather x1, waiting for transfers between devices, per_device(): lax.all_gather(full_student, 'row', axis=0, tiled=True)  41.9 us
    psum x1, blocking collectives, per_device(): lax.psum((sum_teacher * teacher_scale, cross_term * teacher_scale, sum_st...  40 us
    pmax x1, blocking collectives, per_device(): lax.pmax((top_teacher, top_student), ('row', 'col'))  39.2 us
    all_gather x1, blocking collectives, per_device(): lax.all_gather(student_hidden, 'col', axis=1, tiled=True)  8.65 us
    all_gather x1, blocking collectives, per_device(): lax.all_gather(teacher_hidden, 'col', axis=1, tiled=True)  6.13 us
    dot_general x1, matrix products, per_device(): jnp.einsum('td,vd->tv', lax.all_gather(full_teacher, 'row', axis=0, tiled...  5.93 us
    dot_general x1, matrix products, per_device(): jnp.einsum('td,vd->tv', lax.all_gather(full_student, 'row', axis=0, tiled...  5.25 us
  transfers between devices with their start and end apart: 2, of which 2 were waited for; matrix products, arithmetic and copies ran while one was open for 2% of the time, Pallas kernels for 0%

commit v1 on v0

--- a/solution.py
+++ b/solution.py
@@ -2,6 +2,45 @@
 import jax.numpy as jnp
 from jax import lax
 from jax.sharding import PartitionSpec as P
+
+
+def spans_open(unit, axis_tag, chunk):
+    spare, plain, v_now = (lax.axis_size(axis_tag), lax.axis_index(axis_tag), unit.shape[0])
+    nodes = []
+    kk = 0
+    while kk < spare:
+        nodes.append((kk, (kk + 1) % spare))
+        kk += 1
+    items = []
+    for d, i in nodes:
+        items.append((i, d))
+    reached, v1 = (
+        lax.ppermute(unit, perm=nodes, axis_name=axis_tag),
+        lax.ppermute(unit, axis_name=axis_tag, perm=items),
+    )
+    block_out = chunk(unit, plain * v_now)
+    carry = block_out.shape[0]
+    w_next = jnp.zeros((*block_out.shape[:0], spare * carry, *block_out.shape[1:]), block_out.dtype)
+
+    def _launch_leaves(w_next, block_out, e_next):
+        b_now = lax.dynamic_update_slice_in_dim(w_next, block_out, e_next * carry, axis=0)
+        return b_now
+
+    w_next = _launch_leaves(w_next, block_out, plain)
+    at = 1
+    while at < spare // 2 + 1:
+        piece_next, high = ((plain - at) % spare, (plain + at) % spare)
+        state_now = (reached, v1)
+        if at < spare // 2:
+            reached, v1 = (
+                lax.ppermute(reached, axis_name=axis_tag, perm=nodes),
+                lax.ppermute(v1, axis_name=axis_tag, perm=items),
+            )
+        w_next = _launch_leaves(w_next, chunk(state_now[0], piece_next * v_now), piece_next)
+        if 2 * at < spare:
+            w_next = _launch_leaves(w_next, chunk(state_now[1], high * v_now), high)
+        at += 1
+    return w_next
 
 
 def block_stats(logit_teacher, logit_student):
@@ -26,11 +65,12 @@
         teacher_embed,
         preferred_element_type=jnp.float32,
     )
-    logit_student = jnp.einsum(
-        "td,vd->tv",
-        lax.all_gather(full_student, "row", axis=0, tiled=True),
-        student_embed,
-        preferred_element_type=jnp.float32,
+    logit_student = spans_open(
+        full_student,
+        "row",
+        lambda own_block_2, start: jnp.einsum(
+            "td,vd->tv", own_block_2, student_embed, preferred_element_type=jnp.float32
+        ),
     )
     current = block_stats(logit_teacher, logit_student)
     partial_stats = tuple((fresh_rows for fresh_rows in current))

time: 214 us -> 240 us (1.12)
  waiting for transfers between devices: 90.8 us -> 7.94 us
  matrix products: 11.2 us -> 56.3 us
  local copies, waits for them, and re-layouts: 0.58 us -> 32.7 us
  starting transfers between devices: 0.08 us -> 32 us
    all_gather x1, waiting for transfers between devices: 48.9 us -> 0.01 us  [per_device(): lax.all_gather(full_teacher, 'row', axis=0, tiled=True)]
    dot_general x1 -> x16, matrix products: 5.25 us -> 50.4 us  [per_device(): jnp.einsum('td,vd->tv', own_block_2, student_embed, preferred_element_typ...]
    all_gather x1 -> x0, waiting for transfers between devices: 41.9 us -> none  [per_device(): lax.all_gather(full_student, 'row', axis=0, tiled=True)]
    dynamic_update_slice x0 -> x16, local copies, waits for them, and re-layouts: none -> 32 us  [_launch_leaves(): lax.dynamic_update_slice_in_dim(w_next, block_out, e_next * carry, axis=0)]
    ppermute x0 -> x15, starting transfers between devices: none -> 31.9 us  [the longest x6 26.9 us: spans_open(): lax.ppermute(v1, axis_name=axis_tag, perm=items)]
    ppermute x0 -> x15, waiting for transfers between devices: none -> 7.91 us  [the longest x6 5.21 us: spans_open(): lax.ppermute(v1, axis_name=axis_tag, perm=items)]
    all_gather x1, blocking collectives: 6.13 us -> 9.37 us  [per_device(): lax.all_gather(teacher_hidden, 'col', axis=1, tiled=True)]
    all_gather x1, blocking collectives: 8.65 us -> 5.67 us  [per_device(): lax.all_gather(student_hidden, 'col', axis=1, tiled=True)]
  transfers between devices with their start and end apart: 2 -> 16, of which waited for: 2 -> 3; matrix products, arithmetic and copies ran while one was open for 2% -> 35% of each run, Pallas kernels for 0% -> 0%
where the time goes in v1:
time: 240 us; the launch traced here: 239 us
  blocking collectives  93 us (39%)
  matrix products  56.3 us (23%)
  local copies, waits for them, and re-layouts  32.7 us (14%)
  starting transfers between devices  32 us (13%)
  between operations  16.2 us (7%)
  waiting for transfers between devices  7.94 us (3%)
    dot_general x16, matrix products, per_device(): jnp.einsum('td,vd->tv', own_block_2, student_embed, preferred_element_typ...  50.4 us
    psum x1, blocking collectives, per_device(): lax.psum((sum_teacher * teacher_scale, cross_term * teacher_scale, sum_st...  41.1 us
    pmax x1, blocking collectives, per_device(): lax.pmax((top_teacher, top_student), ('row', 'col'))  36.8 us
    dynamic_update_slice x16, local copies, waits for them, and re-layouts, _launch_leaves(): lax.dynamic_update_slice_in_dim(w_next, block_out, e_next * carry, axis=0)  32 us
    ppermute x6, starting transfers between devices, spans_open(): lax.ppermute(v1, axis_name=axis_tag, perm=items)  26.9 us
    all_gather x1, blocking collectives, per_device(): lax.all_gather(teacher_hidden, 'col', axis=1, tiled=True)  9.37 us
    dot_general x1, matrix products, per_device(): jnp.einsum('td,vd->tv', lax.all_gather(full_teacher, 'row', axis=0, tiled...  5.95 us
    all_gather x1, blocking collectives, per_device(): lax.all_gather(student_hidden, 'col', axis=1, tiled=True)  5.67 us
  transfers between devices with their start and end apart: 16, of which 3 were waited for; matrix products, arithmetic and copies ran while one was open for 35% of the time, Pallas kernels for 0%

profile of v1, /device:TPU:0, one launch (start us, length us, event | category | flops | bytes accessed | tf_op | source)
XLA Modules:
  0.0 239.2 jit_solution(16968696900047661427)
XLA Ops:
  7.2 9.4 %all_gather.9 = bf16[32,4608]{1,0:T(8,128)(2,1)} all-gather(bf16[32,2304]{1,0:T(8,128)(2,1)} %param.4), channel_id=1, replica_groups=mesh['row'=16,'col'=2] {'col'}, dimensions={1}, use_global_device_ids=true | all-gather | bytes 442368 | tf_op jit(solution)/shard_map/all_gather | solution.py:59
  16.6 5.7 %all_gather.11 = bf16[32,3584]{1,0:T(8,128)(2,1)S(1)} all-gather(bf16[32,1792]{1,0:T(8,128)(2,1)} %param.5), channel_id=1, replica_groups=mesh['row'=16,'col'=2] {'col'}, dimensions={1}, use_global_device_ids=true | all-gather | bytes 344064 | tf_op jit(solution)/shard_map/all_gather | solution.py:60
  22.3 4.4 %collective-permute-start.1 = (bf16[32,3584]{1,0:T(8,128)(2,1)S(1)}, bf16[32,3584]{1,0:T(8,128)(2,1)S(1)}, u32[]{:S(2)}, u32[]{:S(2)}) collective-permute-start(bf16[32,3584]{1,0:T(8,128)(2,1)S(1)} %all_gather.11), channel_id=1, source_target_pairs={{2,0},{4,2},{6,4},{8,6},{10,8},{12,10},{14,12},{16,14},{18,16},{20... | collective-permute-start | bytes 688136 | tf_op jit(solution)/shard_map/ppermute | solution.py:19
  26.7 3.1 %fusion.5 = f32[32,512]{0,1:T(8,128)S(1)} fusion(bf16[32,3584]{1,0:T(8,128)(2,1)S(1)} %all_gather.11, bf16[512,3584]{1,0:T(8,128)(2,1)} %param.7), kind=kOutput, calls=%fused_computation.11 | convolution fusion | flops 117440512 | bytes 3964928 | tf_op jit(solution)/shard_map/td,vd->tv/dot_general | solution.py:71
  30.0 1.9 dynamic_update_slice.48
  31.9 3.1 %fusion.6 = f32[32,512]{0,1:T(8,128)S(1)} fusion(bf16[32,3584]{1,0:T(8,128)(2,1)S(1)} %collective-permute-done, bf16[512,3584]{1,0:T(8,128)(2,1)} %param.7), kind=kOutput, calls=%fused_computation.12 | convolution fusion | flops 117440512 | bytes 3964928 | tf_op jit(solution)/shard_map/td,vd->tv/dot_general | solution.py:71
  35.0 1.5 dynamic_update_slice.49
  36.6 3.1 %fusion.7 = f32[32,512]{0,1:T(8,128)S(1)} fusion(bf16[32,3584]{1,0:T(8,128)(2,1)S(1)} %collective-permute-done.1, bf16[512,3584]{1,0:T(8,128)(2,1)} %param.7), kind=kOutput, calls=%fused_computation.13 | convolution fusion | flops 117440512 | bytes 3964928 | tf_op jit(solution)/shard_map/td,vd->tv/dot_general | solution.py:71
  39.7 2.3 dynamic_update_slice.50
  42.0 4.1 %collective-permute-start.3 = (bf16[32,3584]{1,0:T(8,128)(2,1)S(1)}, bf16[32,3584]{1,0:T(8,128)(2,1)S(1)}, u32[]{:S(2)}, u32[]{:S(2)}) collective-permute-start(bf16[32,3584]{1,0:T(8,128)(2,1)S(1)} %collective-permute-done.1), channel_id=1, source_target_pairs={{2,0},{4,2},{6,4},{8,6},{10,8},{12,10},{14,12},{16,14},{18,16},{20... | collective-permute-start | bytes 688136 | tf_op jit(solution)/shard_map/ppermute | solution.py:37
  46.1 3.7 %fusion.8 = f32[32,512]{0,1:T(8,128)S(1)} fusion(bf16[32,3584]{1,0:T(8,128)(2,1)S(1)} %collective-permute-done.2, bf16[512,3584]{1,0:T(8,128)(2,1)} %param.7), kind=kOutput, calls=%fused_computation.14 | convolution fusion | flops 117440512 | bytes 3964928 | tf_op jit(solution)/shard_map/td,vd->tv/dot_general | solution.py:71
  49.8 1.5 dynamic_update_slice.51
  51.3 3.0 %collective-permute-done.3 = bf16[32,3584]{1,0:T(8,128)(2,1)S(1)} collective-permute-done((bf16[32,3584]{1,0:T(8,128)(2,1)S(1)}, bf16[32,3584]{1,0:T(8,128)(2,1)S(1)}, u32[]{:S(2)}, u32[]{:S(2)}) %collective-permute-start.3) | collective-permute-done | bytes 229408 | tf_op jit(solution)/shard_map/ppermute | solution.py:37
  54.3 3.1 %fusion.9 = f32[32,512]{0,1:T(8,128)S(1)} fusion(bf16[32,3584]{1,0:T(8,128)(2,1)S(1)} %collective-permute-done.3, bf16[512,3584]{1,0:T(8,128)(2,1)} %param.7), kind=kOutput, calls=%fused_computation.15 | convolution fusion | flops 117440512 | bytes 3964928 | tf_op jit(solution)/shard_map/td,vd->tv/dot_general | solution.py:71
  57.4 2.3 dynamic_update_slice.52
  59.7 4.7 %collective-permute-start.5 = (bf16[32,3584]{1,0:T(8,128)(2,1)S(1)}, bf16[32,3584]{1,0:T(8,128)(2,1)S(1)}, u32[]{:S(2)}, u32[]{:S(2)}) collective-permute-start(bf16[32,3584]{1,0:T(8,128)(2,1)S(1)} %collective-permute-done.3), channel_id=1, source_target_pairs={{2,0},{4,2},{6,4},{8,6},{10,8},{12,10},{14,12},{16,14},{18,16},{20... | collective-permute-start | bytes 688136 | tf_op jit(solution)/shard_map/ppermute | solution.py:37
  64.4 3.1 %fusion.10 = f32[32,512]{0,1:T(8,128)S(1)} fusion(bf16[32,3584]{1,0:T(8,128)(2,1)S(1)} %collective-permute-done.4, bf16[512,3584]{1,0:T(8,128)(2,1)} %param.7), kind=kOutput, calls=%fused_computation.16 | convolution fusion | flops 117440512 | bytes 3964928 | tf_op jit(solution)/shard_map/td,vd->tv/dot_general | solution.py:71
  67.5 1.5 dynamic_update_slice.53
  69.0 2.2 collective-permute-done.5
  71.3 3.1 %fusion.11 = f32[32,512]{0,1:T(8,128)S(1)} fusion(bf16[32,3584]{1,0:T(8,128)(2,1)S(1)} %collective-permute-done.5, bf16[512,3584]{1,0:T(8,128)(2,1)} %param.7), kind=kOutput, calls=%fused_computation.17 | convolution fusion | flops 117440512 | bytes 3964928 | tf_op jit(solution)/shard_map/td,vd->tv/dot_general | solution.py:71
  74.4 2.3 dynamic_update_slice.54
  76.7 4.7 %collective-permute-start.7 = (bf16[32,3584]{1,0:T(8,128)(2,1)S(1)}, bf16[32,3584]{1,0:T(8,128)(2,1)S(1)}, u32[]{:S(2)}, u32[]{:S(2)}) collective-permute-start(bf16[32,3584]{1,0:T(8,128)(2,1)S(1)} %collective-permute-done.5), channel_id=1, source_target_pairs={{2,0},{4,2},{6,4},{8,6},{10,8},{12,10},{14,12},{16,14},{18,16},{20... | collective-permute-start | bytes 688136 | tf_op jit(solution)/shard_map/ppermute | solution.py:37
  81.4 3.1 %fusion.12 = f32[32,512]{0,1:T(8,128)S(1)} fusion(bf16[32,3584]{1,0:T(8,128)(2,1)S(1)} %collective-permute-done.6, bf16[512,3584]{1,0:T(8,128)(2,1)} %param.7), kind=kOutput, calls=%fused_computation.18 | convolution fusion | flops 117440512 | bytes 3964928 | tf_op jit(solution)/shard_map/td,vd->tv/dot_general | solution.py:71
  84.5 1.1 dynamic_update_slice.55
  85.7 3.1 %fusion.13 = f32[32,512]{0,1:T(8,128)S(1)} fusion(bf16[32,3584]{1,0:T(8,128)(2,1)S(1)} %collective-permute-done.7, bf16[512,3584]{1,0:T(8,128)(2,1)} %param.7), kind=kOutput, calls=%fused_computation.19 | convolution fusion | flops 117440512 | bytes 3964928 | tf_op jit(solution)/shard_map/td,vd->tv/dot_general | solution.py:71
  88.8 1.9 dynamic_update_slice.56
  90.7 4.9 %collective-permute-start.9 = (bf16[32,3584]{1,0:T(8,128)(2,1)S(1)}, bf16[32,3584]{1,0:T(8,128)(2,1)S(1)}, u32[]{:S(2)}, u32[]{:S(2)}) collective-permute-start(bf16[32,3584]{1,0:T(8,128)(2,1)S(1)} %collective-permute-done.7), channel_id=1, source_target_pairs={{2,0},{4,2},{6,4},{8,6},{10,8},{12,10},{14,12},{16,14},{18,16},{20... | collective-permute-start | bytes 688136 | tf_op jit(solution)/shard_map/ppermute | solution.py:37
  95.6 3.1 %fusion.14 = f32[32,512]{0,1:T(8,128)S(1)} fusion(bf16[32,3584]{1,0:T(8,128)(2,1)S(1)} %collective-permute-done.8, bf16[512,3584]{1,0:T(8,128)(2,1)} %param.7), kind=kOutput, calls=%fused_computation.20 | convolution fusion | flops 117440512 | bytes 3964928 | tf_op jit(solution)/shard_map/td,vd->tv/dot_general | solution.py:71
  98.7 2.3 dynamic_update_slice.57
  101.3 3.1 %fusion.15 = f32[32,512]{0,1:T(8,128)S(1)} fusion(bf16[32,3584]{1,0:T(8,128)(2,1)S(1)} %collective-permute-done.9, bf16[512,3584]{1,0:T(8,128)(2,1)} %param.7), kind=kOutput, calls=%fused_computation.21 | convolution fusion | flops 117440512 | bytes 3964928 | tf_op jit(solution)/shard_map/td,vd->tv/dot_general | solution.py:71
  104.4 2.3 dynamic_update_slice.58
  106.7 4.1 %collective-permute-start.11 = (bf16[32,3584]{1,0:T(8,128)(2,1)S(1)}, bf16[32,3584]{1,0:T(8,128)(2,1)S(1)}, u32[]{:S(2)}, u32[]{:S(2)}) collective-permute-start(bf16[32,3584]{1,0:T(8,128)(2,1)S(1)} %collective-permute-done.9), channel_id=1, source_target_pairs={{2,0},{4,2},{6,4},{8,6},{10,8},{12,10},{14,12},{16,14},{18,16},{20... | collective-permute-start | bytes 688136 | tf_op jit(solution)/shard_map/ppermute | solution.py:37
  110.8 3.1 %fusion.16 = f32[32,512]{0,1:T(8,128)S(1)} fusion(bf16[32,3584]{1,0:T(8,128)(2,1)S(1)} %collective-permute-done.10, bf16[512,3584]{1,0:T(8,128)(2,1)} %param.7), kind=kOutput, calls=%fused_computation.22 | convolution fusion | flops 117440512 | bytes 3964928 | tf_op jit(solution)/shard_map/td,vd->tv/dot_general | solution.py:71
  113.9 2.3 dynamic_update_slice.59
  116.3 3.1 %fusion.17 = f32[32,512]{0,1:T(8,128)S(1)} fusion(bf16[32,3584]{1,0:T(8,128)(2,1)S(1)} %collective-permute-done.11, bf16[512,3584]{1,0:T(8,128)(2,1)} %param.7), kind=kOutput, calls=%fused_computation.23 | convolution fusion | flops 117440512 | bytes 3964928 | tf_op jit(solution)/shard_map/td,vd->tv/dot_general | solution.py:71
  119.4 2.3 dynamic_update_slice.60
  121.8 4.5 %collective-permute-start.13 = (bf16[32,3584]{1,0:T(8,128)(2,1)S(1)}, bf16[32,3584]{1,0:T(8,128)(2,1)S(1)}, u32[]{:S(2)}, u32[]{:S(2)}) collective-permute-start(bf16[32,3584]{1,0:T(8,128)(2,1)S(1)} %collective-permute-done.11), channel_id=1, source_target_pairs={{2,0},{4,2},{6,4},{8,6},{10,8},{12,10},{14,12},{16,14},{18,16},{20... | collective-permute-start | bytes 688136 | tf_op jit(solution)/shard_map/ppermute | solution.py:37
  126.2 3.1 %fusion.18 = f32[32,512]{0,1:T(8,128)S(1)} fusion(bf16[32,3584]{1,0:T(8,128)(2,1)S(1)} %collective-permute-done.12, bf16[512,3584]{1,0:T(8,128)(2,1)} %param.7), kind=kOutput, calls=%fused_computation.24 | convolution fusion | flops 117440512 | bytes 3964928 | tf_op jit(solution)/shard_map/td,vd->tv/dot_general | solution.py:71
  129.4 2.3 dynamic_update_slice.61
  131.8 3.1 %fusion.19 = f32[32,512]{0,1:T(8,128)S(1)} fusion(bf16[32,3584]{1,0:T(8,128)(2,1)S(1)} %collective-permute-done.13, bf16[512,3584]{1,0:T(8,128)(2,1)} %param.7), kind=kOutput, calls=%fused_computation.25 | convolution fusion | flops 117440512 | bytes 3964928 | tf_op jit(solution)/shard_map/td,vd->tv/dot_general | solution.py:71
  134.9 2.3 dynamic_update_slice.62
  137.2 2.7 %collective-permute-done.14 = bf16[32,3584]{1,0:T(8,128)(2,1)S(1)} collective-permute-done((bf16[32,3584]{1,0:T(8,128)(2,1)S(1)}, bf16[32,3584]{1,0:T(8,128)(2,1)S(1)}, u32[]{:S(2)}, u32[]{:S(2)}) %collective-permute-start.14) | collective-permute-done | bytes 229408 | tf_op jit(solution)/shard_map/ppermute | solution.py:36
  139.9 3.1 %fusion.20 = f32[32,512]{0,1:T(8,128)S(1)} fusion(bf16[32,3584]{1,0:T(8,128)(2,1)S(1)} %collective-permute-done.14, bf16[512,3584]{1,0:T(8,128)(2,1)} %param.7), kind=kOutput, calls=%fused_computation.26 | convolution fusion | flops 117440512 | bytes 3964928 | tf_op jit(solution)/shard_map/td,vd->tv/dot_general | solution.py:71
  143.0 1.9 dynamic_update_slice.63
  145.0 5.9 %fusion.4 = (f32[512]{0:T(512)S(1)}, f32[512,512]{0,1:T(8,128)S(1)}) fusion(bf16[512,4608]{1,0:T(8,128)(2,1)} %all-gather.2.cloned.1.call-done, bf16[512,4608]{1,0:T(8,128)(2,1)} %param.6), kind=kOutput, calls=%fused_computation.10 | convolution fusion | flops 2416180736 | bytes 10487808 | tf_op jit(solution)/shard_map/td,vd->tv/dot_general | solution.py:62
  151.0 36.8 %all-reduce.1 = (f32[512]{0:T(512)S(1)}, f32[512]{0:T(512)S(1)}) all-reduce(f32[512]{0:T(512)S(1)} %reduce_max.19, f32[512]{0:T(512)S(1)} %get-tuple-element.14), channel_id=1, replica_groups=mesh['row'=16,'col'=2] {'row','col'}, use_global_device_ids=true, to_apply=%region_7.8 | all-reduce | flops 1024 | bytes 8192 | tf_op jit(solution)/shard_map/pmax | solution.py:78
  188.3 41.1 %all-reduce = (f32[512]{0:T(512)S(1)}, f32[512]{0:T(512)S(1)}, f32[512]{0:T(512)S(1)}) all-reduce(f32[512]{0:T(512)S(1)} %get-tuple-element.16, f32[512]{0:T(512)S(1)} %get-tuple-element.13, f32[512]{0:T(512)S(1)} %get-tuple-element.12), channel_id=1, replica_groups=mesh['row'=16,'col'=2] {'row','col'}, use_global_device_ids=true, to_apply=%region_9.10 | all-reduce | flops 1536 | bytes 12288 | tf_op jit(solution)/shard_map/psum | solution.py:81
  229.4 0.6 fusion.3
  (28 shorter events, 1.9 us)
Async XLA Ops:
  7.2 137.9 %all-gather.2.cloned.1.call-start = ((), (), s32[]{:S(2)}) async-start(), calls=%async_computation | async-start | bytes 5013504 | tf_op jit(solution)/shard_map/all_gather | solution.py:64
  22.3 9.6 %collective-permute-start = (bf16[32,3584]{1,0:T(8,128)(2,1)S(1)}, bf16[32,3584]{1,0:T(8,128)(2,1)S(1)}, u32[]{:S(2)}, u32[]{:S(2)}) collective-permute-start(bf16[32,3584]{1,0:T(8,128)(2,1)S(1)} %all_gather.11), channel_id=1, source_target_pairs={{0,2},{2,4},{4,6},{6,8},{8,10},{10,12},{12,14},{14,16},{16,18},{18... | collective-permute-start | bytes 688136 | tf_op jit(solution)/shard_map/ppermute | solution.py:18
  22.3 14.3 %collective-permute-start.1 = (bf16[32,3584]{1,0:T(8,128)(2,1)S(1)}, bf16[32,3584]{1,0:T(8,128)(2,1)S(1)}, u32[]{:S(2)}, u32[]{:S(2)}) collective-permute-start(bf16[32,3584]{1,0:T(8,128)(2,1)S(1)} %all_gather.11), channel_id=1, source_target_pairs={{2,0},{4,2},{6,4},{8,6},{10,8},{12,10},{14,12},{16,14},{18,16},{20... | collective-permute-start | bytes 688136 | tf_op jit(solution)/shard_map/ppermute | solution.py:19
  36.5 9.6 %collective-permute-start.2 = (bf16[32,3584]{1,0:T(8,128)(2,1)S(1)}, bf16[32,3584]{1,0:T(8,128)(2,1)S(1)}, u32[]{:S(2)}, u32[]{:S(2)}) collective-permute-start(bf16[32,3584]{1,0:T(8,128)(2,1)S(1)} %collective-permute-done), channel_id=1, source_target_pairs={{0,2},{2,4},{4,6},{6,8},{8,10},{10,12},{12,14},{14,16},{16,18},{18... | collective-permute-start | bytes 688136 | tf_op jit(solution)/shard_map/ppermute | solution.py:36
  42.0 12.3 %collective-permute-start.3 = (bf16[32,3584]{1,0:T(8,128)(2,1)S(1)}, bf16[32,3584]{1,0:T(8,128)(2,1)S(1)}, u32[]{:S(2)}, u32[]{:S(2)}) collective-permute-start(bf16[32,3584]{1,0:T(8,128)(2,1)S(1)} %collective-permute-done.1), channel_id=1, source_target_pairs={{2,0},{4,2},{6,4},{8,6},{10,8},{12,10},{14,12},{16,14},{18,16},{20... | collective-permute-start | bytes 688136 | tf_op jit(solution)/shard_map/ppermute | solution.py:37
  51.2 13.2 %collective-permute-start.4 = (bf16[32,3584]{1,0:T(8,128)(2,1)S(1)}, bf16[32,3584]{1,0:T(8,128)(2,1)S(1)}, u32[]{:S(2)}, u32[]{:S(2)}) collective-permute-start(bf16[32,3584]{1,0:T(8,128)(2,1)S(1)} %collective-permute-done.2), channel_id=1, source_target_pairs={{0,2},{2,4},{4,6},{6,8},{8,10},{10,12},{12,14},{14,16},{16,18},{18... | collective-permute-start | bytes 688136 | tf_op jit(solution)/shard_map/ppermute | solution.py:36
  59.7 11.5 %collective-permute-start.5 = (bf16[32,3584]{1,0:T(8,128)(2,1)S(1)}, bf16[32,3584]{1,0:T(8,128)(2,1)S(1)}, u32[]{:S(2)}, u32[]{:S(2)}) collective-permute-start(bf16[32,3584]{1,0:T(8,128)(2,1)S(1)} %collective-permute-done.3), channel_id=1, source_target_pairs={{2,0},{4,2},{6,4},{8,6},{10,8},{12,10},{14,12},{16,14},{18,16},{20... | collective-permute-start | bytes 688136 | tf_op jit(solution)/shard_map/ppermute | solution.py:37
  69.0 12.4 %collective-permute-start.6 = (bf16[32,3584]{1,0:T(8,128)(2,1)S(1)}, bf16[32,3584]{1,0:T(8,128)(2,1)S(1)}, u32[]{:S(2)}, u32[]{:S(2)}) collective-permute-start(bf16[32,3584]{1,0:T(8,128)(2,1)S(1)} %collective-permute-done.4), channel_id=1, source_target_pairs={{0,2},{2,4},{4,6},{6,8},{8,10},{10,12},{12,14},{14,16},{16,18},{18... | collective-permute-start | bytes 688136 | tf_op jit(solution)/shard_map/ppermute | solution.py:36
  76.7 9.0 %collective-permute-start.7 = (bf16[32,3584]{1,0:T(8,128)(2,1)S(1)}, bf16[32,3584]{1,0:T(8,128)(2,1)S(1)}, u32[]{:S(2)}, u32[]{:S(2)}) collective-permute-start(bf16[32,3584]{1,0:T(8,128)(2,1)S(1)} %collective-permute-done.5), channel_id=1, source_target_pairs={{2,0},{4,2},{6,4},{8,6},{10,8},{12,10},{14,12},{16,14},{18,16},{20... | collective-permute-start | bytes 688136 | tf_op jit(solution)/shard_map/ppermute | solution.py:37
  85.6 10.0 %collective-permute-start.8 = (bf16[32,3584]{1,0:T(8,128)(2,1)S(1)}, bf16[32,3584]{1,0:T(8,128)(2,1)S(1)}, u32[]{:S(2)}, u32[]{:S(2)}) collective-permute-start(bf16[32,3584]{1,0:T(8,128)(2,1)S(1)} %collective-permute-done.6), channel_id=1, source_target_pairs={{0,2},{2,4},{4,6},{6,8},{8,10},{10,12},{12,14},{14,16},{16,18},{18... | collective-permute-start | bytes 688136 | tf_op jit(solution)/shard_map/ppermute | solution.py:36
  90.7 10.5 %collective-permute-start.9 = (bf16[32,3584]{1,0:T(8,128)(2,1)S(1)}, bf16[32,3584]{1,0:T(8,128)(2,1)S(1)}, u32[]{:S(2)}, u32[]{:S(2)}) collective-permute-start(bf16[32,3584]{1,0:T(8,128)(2,1)S(1)} %collective-permute-done.7), channel_id=1, source_target_pairs={{2,0},{4,2},{6,4},{8,6},{10,8},{12,10},{14,12},{16,14},{18,16},{20... | collective-permute-start | bytes 688136 | tf_op jit(solution)/shard_map/ppermute | solution.py:37
  101.0 9.8 %collective-permute-start.10 = (bf16[32,3584]{1,0:T(8,128)(2,1)S(1)}, bf16[32,3584]{1,0:T(8,128)(2,1)S(1)}, u32[]{:S(2)}, u32[]{:S(2)}) collective-permute-start(bf16[32,3584]{1,0:T(8,128)(2,1)S(1)} %collective-permute-done.8), channel_id=1, source_target_pairs={{0,2},{2,4},{4,6},{6,8},{8,10},{10,12},{12,14},{14,16},{16,18},{18... | collective-permute-start | bytes 688136 | tf_op jit(solution)/shard_map/ppermute | solution.py:36
  106.7 9.6 %collective-permute-start.11 = (bf16[32,3584]{1,0:T(8,128)(2,1)S(1)}, bf16[32,3584]{1,0:T(8,128)(2,1)S(1)}, u32[]{:S(2)}, u32[]{:S(2)}) collective-permute-start(bf16[32,3584]{1,0:T(8,128)(2,1)S(1)} %collective-permute-done.9), channel_id=1, source_target_pairs={{2,0},{4,2},{6,4},{8,6},{10,8},{12,10},{14,12},{16,14},{18,16},{20... | collective-permute-start | bytes 688136 | tf_op jit(solution)/shard_map/ppermute | solution.py:37
  116.2 10.0 %collective-permute-start.12 = (bf16[32,3584]{1,0:T(8,128)(2,1)S(1)}, bf16[32,3584]{1,0:T(8,128)(2,1)S(1)}, u32[]{:S(2)}, u32[]{:S(2)}) collective-permute-start(bf16[32,3584]{1,0:T(8,128)(2,1)S(1)} %collective-permute-done.10), channel_id=1, source_target_pairs={{0,2},{2,4},{4,6},{6,8},{8,10},{10,12},{12,14},{14,16},{16,18},{18... | collective-permute-start | bytes 688136 | tf_op jit(solution)/shard_map/ppermute | solution.py:36
  121.8 10.0 %collective-permute-start.13 = (bf16[32,3584]{1,0:T(8,128)(2,1)S(1)}, bf16[32,3584]{1,0:T(8,128)(2,1)S(1)}, u32[]{:S(2)}, u32[]{:S(2)}) collective-permute-start(bf16[32,3584]{1,0:T(8,128)(2,1)S(1)} %collective-permute-done.11), channel_id=1, source_target_pairs={{2,0},{4,2},{6,4},{8,6},{10,8},{12,10},{14,12},{16,14},{18,16},{20... | collective-permute-start | bytes 688136 | tf_op jit(solution)/shard_map/ppermute | solution.py:37
  131.7 8.2 %collective-permute-start.14 = (bf16[32,3584]{1,0:T(8,128)(2,1)S(1)}, bf16[32,3584]{1,0:T(8,128)(2,1)S(1)}, u32[]{:S(2)}, u32[]{:S(2)}) collective-permute-start(bf16[32,3584]{1,0:T(8,128)(2,1)S(1)} %collective-permute-done.12), channel_id=1, source_target_pairs={{0,2},{2,4},{4,6},{6,8},{8,10},{10,12},{12,14},{14,16},{16,18},{18... | collective-permute-start | bytes 688136 | tf_op jit(solution)/shard_map/ppermute | solution.py:36
Sparse Core Ops, SparseCore 0:
  16.7 62.1 all-gather.1
